TPU v7x, 256 devices: a whole 4x4x8 slice. The times are simulated.
256 devices in a mesh: tile: 8 (over y, core), freq: 32 (over x, z).
Axes of the slice: x: 4, y: 4, z: 8, core: 2. Of those that a mesh axis runs over, the one named last changes fastest.
Arguments:
- sensitivity: float32 [8, 32, 2, 1024, 512], P('tile', 'freq'), may hold values from -0.25 to 0.25
- models: float32 [2048, 256], P(('tile', 'freq')), may hold values from -6 to 6
- observed: float32 [8, 40, 1024], P('tile', None, 'freq'), may hold values from -6 to 6
- waveform: float32 [128], replicated, may hold values from -0.5 to 0.5
- cell_index: int32 [8, 512], P('tile'), may hold values from 0 to 2047, as said below
- gate_index: int32 [40], replicated, may hold values from 10 to 127, as said below
Outputs:
- updated: float32 [2048, 256], P(('tile', 'freq'))
- misfit: float32 [256], replicated
Inputs may be any that keep to these rules, and one draw needn't show every extreme that they name: `cell_index`: each tile's indices are distinct. Tile t holds, in some order, the 256 global cells from t * 256 on and the 256 cells of one other tile's block (from u * 256 on, u != t). Every global cell belongs to one or more tiles. `gate_index`: strictly increasing; the last gate is sample 128 - 1.
All inputs are finite; a program needn't handle non-finite values.
Results may differ from a plain program's by a relative error of at most 0.00017.
Values sent between devices are 32-bit elements; how exact they have to be, the bound alone decides.
A program may use at most 64 MiB of HBM per device.

v0:
```python
import math
import jax
import jax.numpy as jnp
from jax import lax
from jax.sharding import PartitionSpec as P

HIGH = lax.Precision.HIGHEST
PHASE_RATE = 0.37
STEP_LENGTH = 0.5
EPSILON = 1e-06


def gate_tables(freqs, waveform, gate_index):
    samples = waveform.shape[0]
    freq_col = jnp.arange(freqs, dtype=jnp.float32)[:, None] + 0.5
    time_row = jnp.arange(samples, dtype=jnp.float32)[None, :] + 0.5
    phases = PHASE_RATE * freq_col * time_row
    kernel = jnp.stack([jnp.cos(phases), jnp.sin(phases)], axis=1) / math.sqrt(freqs)
    time_lag = jnp.arange(samples)[:, None] - jnp.arange(samples)[None, :]
    toeplitz = jnp.where(time_lag >= 0, jnp.take(waveform, jnp.clip(time_lag, 0, samples - 1)), 0.0)
    picker = (gate_index[:, None] == jnp.arange(samples)[None, :]).astype(jnp.float32)
    return (kernel, toeplitz, picker)


def body(sensitivity, models, observed, waveform, cell_index, gate_index):
    freqs = sensitivity.shape[1] * lax.axis_size("freq")
    soundings = sensitivity.shape[3]
    members = models.shape[1]
    gates = gate_index.shape[0]
    devices = lax.axis_size(("tile", "freq"))
    owned_count = models.shape[0]
    ncells = owned_count * devices
    total = lax.axis_size("tile") * soundings * gates
    kernel, toeplitz, picker = gate_tables(freqs, waveform, gate_index)
    block = sensitivity[0]
    all_models = lax.all_gather(models, ("tile", "freq"), axis=0, tiled=True)
    tile_cells = cell_index[0]
    tile_models = jnp.take(all_models, tile_cells, axis=0)
    predicted = jnp.einsum("fpsc,cm->fpsm", block, tile_models, precision=HIGH)
    spectra = lax.all_to_all(predicted, "freq", split_axis=2, concat_axis=0, tiled=True)
    series = jnp.einsum("fpk,fpsm->ksm", kernel, spectra, precision=HIGH)
    series = jnp.einsum("kj,jsm->ksm", toeplitz, series, precision=HIGH)
    response = jnp.einsum("gk,ksm->gsm", picker, series, precision=HIGH)
    misfit_rows = response - observed[0][:, :, None]
    partial_misfit = jnp.sum(misfit_rows * misfit_rows, axis=(0, 1))
    misfit_total = lax.psum(partial_misfit, ("tile", "freq"))
    upward = jnp.einsum("gk,gsm->ksm", picker, misfit_rows, precision=HIGH)
    upward = jnp.einsum("kj,ksm->jsm", toeplitz, upward, precision=HIGH)
    back = jnp.einsum("fpk,ksm->fpsm", kernel, upward, precision=HIGH)
    back_spectra = lax.all_to_all(back, "freq", split_axis=0, concat_axis=2, tiled=True)
    cell_terms = jnp.einsum("fpsc,fpsm->cm", block, back_spectra, precision=HIGH)
    scattered = jnp.zeros((ncells, members), jnp.float32).at[tile_cells].add(cell_terms)
    summed = lax.psum(scattered, ("tile", "freq"))
    gradient = lax.dynamic_slice_in_dim(
        summed, lax.axis_index(("tile", "freq")) * owned_count, owned_count, 0
    )
    partial_square = jnp.sum(gradient * gradient, axis=0)
    square_total = lax.psum(partial_square, ("tile", "freq"))
    misfit = misfit_total / (2.0 * total)
    scale = jnp.sqrt(square_total / ncells + EPSILON)
    updated = models - STEP_LENGTH * (misfit / scale)[None, :] * gradient
    return (updated, misfit)


def solution(mesh):
    in_specs = (
        P("tile", "freq", None, None, None),
        P(("tile", "freq"), None),
        P("tile", None, "freq"),
        P(),
        P("tile", None),
        P(),
    )
    out_specs = (P(("tile", "freq"), None), P())
    return jax.shard_map(body, mesh=mesh, in_specs=in_specs, out_specs=out_specs, check_vma=False)
```

profile of v0, /device:TPU:1, one launch (start us, length us, event | category | flops | bytes accessed | tf_op | source)
XLA Modules:
  0.0 677.4 jit_solution(5995075499652823662)
XLA Ops:
  7.2 0.0 copy-start
  7.2 0.0 all-gather.2.cloned.1.call-start
  7.2 0.7 all-gather.2.cloned.1.call-update
  7.9 0.7 compare_select_fusion.2
  8.6 0.7 compare_and_fusion
  9.3 110.7 %all-gather.2.cloned.1.call-done = f32[2048,256]{1,0:T(8,128)} async-done(((f32[8,256]{1,0:T(8,128)}), f32[2048,256]{1,0:T(8,128)}) %all-gather.2.cloned.1.call-update) | async-done | bytes 2097168 | tf_op jit(solution)/shard_map/all_gather | solution.py:36
  120.0 3.2 gather_fusion.1
  123.2 9.0 %fusion.11 = f32[1,2,1024,256]{2,3,1,0:T(8,128)S(1)} fusion(f32[1,1,2,1024,512]{4,3,2,1,0:T(8,128)} %param.6, f32[512,256]{1,0:T(8,128)S(1)} %gather_fusion.1, pred[512]{0:T(512)(128)(4,1)S(1)} %compare_and_fusion), kind=kOutput, calls=%fused_computation.14 | convolution fusion | flops 3221356544 | bytes 6816256 | tf_op jit(solution)/shard_map/fpsc,cm->fpsm/dot_general | solution.py:39
  132.2 2.4 copy.25
  134.6 7.4 %all-to-all-start = ((f32[1,2,1024,256]{3,1,0,2:T(2,128)}), f32[1,2,1024,256]{3,1,0,2:T(2,128)S(1)}, u32[]{:S(2)}, u32[]{:S(2)}) async-start(f32[1,2,1024,256]{3,1,0,2:T(2,128)} %copy.25), calls=%async_computation | async-start | bytes 4194304 | tf_op jit(solution)/shard_map/all_to_all | solution.py:40
  142.0 0.0 all-reduce.3.cloned.1.call-start
  142.1 97.4 %gather_fusion = f32[16384]{0:T(1024)S(1)} fusion(f32[128]{0:T(128)S(1)} %copy-done, s32[16384]{0:T(1024)S(1)} %fusion.24), kind=kCustom, calls=%fused_computation | custom fusion | bytes 196608 | tf_op jit(solution)/shard_map/jit(_take)/gather | solution.py:20
  239.5 0.1 multiply_cosine_fusion
  239.7 4.7 fusion.8
  244.3 4.0 fusion.2
  248.4 1.9 multiply_reduce_fusion
  250.3 1.9 fusion.38
  252.2 4.3 fusion.25
  256.5 2.3 fusion
  258.8 1.2 copy.29
  260.1 56.3 %all_to_all.33 = f32[32,2,32,256]{3,2,1,0:T(8,128)S(1)} all-to-all(f32[32,2,32,256]{3,2,1,0:T(8,128)S(1)} %copy.29), channel_id=1, replica_groups=mesh['tile'=8,'freq'=32] {'freq'}, dimensions={0} | all-to-all | bytes 4194304 | tf_op jit(solution)/shard_map/all_to_all | solution.py:50
  316.3 0.2 copy.30
  316.6 1.9 copy-done.1
  318.5 3.8 fusion.14
  322.4 0.2 copy.32
  322.6 4.7 scatter_custom_fusion
  327.3 0.0 all-reduce.3.cloned.1.call-update
  327.3 263.0 %all-reduce.3.cloned.1.call-done = f32[2048,256]{1,0:T(8,128)} async-done(((f32[2048,256]{1,0:T(8,128)}), f32[2048,256]{1,0:T(8,128)}) %all-reduce.3.cloned.1.call-update) | async-done | bytes 2097168 | tf_op jit(solution)/shard_map/psum | solution.py:53
  590.3 0.7 multiply_reduce_fusion.1
  591.0 77.7 %all-reduce = (f32[256]{0:T(256)S(1)}, f32[256]{0:T(256)S(1)}) all-reduce(f32[256]{0:T(256)S(1)} %get-tuple-element.8, f32[256]{0:T(256)S(1)} %multiply_reduce_fusion.1), channel_id=1, replica_groups=mesh['tile'=8,'freq'=32] {'tile','freq'}, use_global_device_ids=true, to_apply=%region_1.2 | all-reduce | flops 512 | bytes 4096 | tf_op jit(solution)/shard_map/psum | solution.py:46
  668.7 0.6 multiply_multiply_fusion
  669.3 1.3 multiply_subtract_fusion
  (13 shorter events, 0.1 us)
Async XLA Ops:
  7.2 134.9 %copy-start = (f32[128]{0:T(128)S(1)}, f32[128]{0:T(128)}, u32[]{:S(2)}) copy-start(f32[128]{0:T(128)} %param.9) | copy-start | bytes 1540
  7.2 112.9 %all-gather.2.cloned.1.call-start = ((), (), s32[]{:S(2)}) async-start(), calls=%async_computation.2 | async-start | bytes 2105344 | tf_op jit(solution)/shard_map/all_gather | solution.py:36
  134.6 105.1 %all-to-all-start = ((f32[1,2,1024,256]{3,1,0,2:T(2,128)}), f32[1,2,1024,256]{3,1,0,2:T(2,128)S(1)}, u32[]{:S(2)}, u32[]{:S(2)}) async-start(f32[1,2,1024,256]{3,1,0,2:T(2,128)} %copy.25), calls=%async_computation | async-start | bytes 4194304 | tf_op jit(solution)/shard_map/all_to_all | solution.py:40
  142.0 448.3 %all-reduce.3.cloned.1.call-start = ((), (), s32[]{:S(2)}) async-start(), calls=%async_computation.3 | async-start | bytes 4194304 | tf_op jit(solution)/shard_map/psum | solution.py:53
  244.3 4.1 copy-start.3
  244.3 4.1 copy-start.4
  316.3 2.2 copy-start.1
  322.6 346.7 %copy-start.2 = (f32[8,256]{1,0:T(8,128)S(1)}, f32[8,256]{1,0:T(8,128)}, u32[]{:S(2)}) copy-start(f32[8,256]{1,0:T(8,128)} %param.7) | copy-start | bytes 24580
Sparse Core Ops, SparseCore 0:
  11.7 108.2 all-gather.1
  327.4 262.8 all-reduce.2
where the time goes:
time: 678 us; the launch traced here: 677 us
  waiting for transfers between devices  374 us (55%)
  blocking collectives  134 us (20%)
  local copies, waits for them, and re-layouts  107 us (16%)
  matrix products  31.9 us (5%)
  between operations  14.2 us (2%)
  other arithmetic  8.85 us (1%)
  starting transfers between devices  7.46 us (1%)
    psum x1, waiting for transfers between devices, body(): summed = lax.psum(scattered, ('tile', 'freq'))  263 us
    all_gather x1, waiting for transfers between devices, body(): all_models = lax.all_gather(models, ('tile', 'freq'), axis=0, tiled=True)  111 us
    gather x1, local copies, waits for them, and re-layouts, gate_tables(): jnp.take(waveform, jnp.clip(time_lag, 0, samples - 1))  97.4 us
    psum x1, blocking collectives, body(): misfit_total = lax.psum(partial_misfit, ('tile', 'freq'))  77.7 us
    all_to_all x1, blocking collectives, body(): lax.all_to_all(back, 'freq', split_axis=0, concat_axis=2, tiled=True)  56.3 us
  transfers between devices with their start and end apart: 3, of which 2 were waited for; matrix products, arithmetic and copies ran while one was open for 15% of the time, Pallas kernels for 0%

commit v1 on v0

--- a/solution.py
+++ b/solution.py
@@ -1,3 +1,4 @@
+import functools
 import math
 import jax
 import jax.numpy as jnp
@@ -8,6 +9,15 @@
 PHASE_RATE = 0.37
 STEP_LENGTH = 0.5
 EPSILON = 1e-06
+
+
+def close_cards(array_in, peer_axis, axis_id):
+    for rr in (peer_axis, axis_id):
+        array_in = lax.psum(array_in, rr)
+    return array_in
+
+
+_produce_signs = functools.partial(close_cards, peer_axis="freq", axis_id="tile")
 
 
 def gate_tables(freqs, waveform, gate_index):
@@ -50,7 +60,7 @@
     back_spectra = lax.all_to_all(back, "freq", split_axis=0, concat_axis=2, tiled=True)
     cell_terms = jnp.einsum("fpsc,fpsm->cm", block, back_spectra, precision=HIGH)
     scattered = jnp.zeros((ncells, members), jnp.float32).at[tile_cells].add(cell_terms)
-    summed = lax.psum(scattered, ("tile", "freq"))
+    summed = _produce_signs(scattered)
     gradient = lax.dynamic_slice_in_dim(
         summed, lax.axis_index(("tile", "freq")) * owned_count, owned_count, 0
     )

time: 678 us -> 639 us (0.942)
  waiting for transfers between devices: 374 us -> 335 us
    psum x1 -> x2, waiting for transfers between devices: 263 us -> 224 us  [close_cards(): array_in = lax.psum(array_in, rr)]
  transfers between devices with their start and end apart: 3 -> 4, of which waited for: 2 -> 3; matrix products, arithmetic and copies ran while one was open for 15% -> 15% of each run, Pallas kernels for 0% -> 0%
where the time goes in v1:
time: 639 us
  waiting for transfers between devices  335 us (52%)
  blocking collectives  135 us (21%)
  local copies, waits for them, and re-layouts  107 us (17%)
  matrix products  31.9 us (5%)
  between operations  13.9 us (2%)
  other arithmetic  8.85 us (1%)
  starting transfers between devices  7.5 us (1%)
    psum x2, waiting for transfers between devices, close_cards(): array_in = lax.psum(array_in, rr)  224 us
    all_gather x1, waiting for transfers between devices, body(): all_models = lax.all_gather(models, ('tile', 'freq'), axis=0, tiled=True)  111 us
    gather x1, local copies, waits for them, and re-layouts, gate_tables(): jnp.take(waveform, jnp.clip(time_lag, 0, samples - 1))  97.4 us
    psum x1, blocking collectives, body(): misfit_total = lax.psum(partial_misfit, ('tile', 'freq'))  78.6 us
    all_to_all x1, blocking collectives, body(): lax.all_to_all(back, 'freq', split_axis=0, concat_axis=2, tiled=True)  56.3 us
  transfers between devices with their start and end apart: 4, of which 3 were waited for; matrix products, arithmetic and copies ran while one was open for 15% of the time, Pallas kernels for 0%

profile of v1, /device:TPU:1, one launch (start us, length us, event | category | flops | bytes accessed | tf_op | source)
XLA Modules:
  0.0 638.7 jit_solution(1573145738057989434)
XLA Ops:
  7.2 0.0 all-gather.2.cloned.1.call-start
  7.2 0.7 all-gather.2.cloned.1.call-update
  7.9 0.7 compare_select_fusion.2
  8.6 0.7 compare_and_fusion
  9.3 110.7 %all-gather.2.cloned.1.call-done = f32[2048,256]{1,0:T(8,128)} async-done(((f32[8,256]{1,0:T(8,128)}), f32[2048,256]{1,0:T(8,128)}) %all-gather.2.cloned.1.call-update) | async-done | bytes 2097168 | tf_op jit(solution)/shard_map/all_gather | solution.py:46
  120.0 3.2 gather_fusion.1
  123.2 9.0 %fusion.11 = f32[1,2,1024,256]{2,3,1,0:T(8,128)S(1)} fusion(f32[1,1,2,1024,512]{4,3,2,1,0:T(8,128)} %param.6, f32[512,256]{1,0:T(8,128)S(1)} %gather_fusion.1, pred[512]{0:T(512)(128)(4,1)S(1)} %compare_and_fusion), kind=kOutput, calls=%fused_computation.14 | convolution fusion | flops 3221356544 | bytes 6816256 | tf_op jit(solution)/shard_map/fpsc,cm->fpsm/dot_general | solution.py:49
  132.2 2.4 copy.25
  134.6 7.4 %all-to-all-start = ((f32[1,2,1024,256]{3,1,0,2:T(2,128)}), f32[1,2,1024,256]{3,1,0,2:T(2,128)S(1)}, u32[]{:S(2)}, u32[]{:S(2)}) async-start(f32[1,2,1024,256]{3,1,0,2:T(2,128)} %copy.25), calls=%async_computation | async-start | bytes 4194304 | tf_op jit(solution)/shard_map/all_to_all | solution.py:50
  142.0 0.0 all-reduce.4.cloned.1.call-start
  142.1 97.4 %gather_fusion = f32[16384]{0:T(1024)S(1)} fusion(f32[128]{0:T(128)S(1)} %copy-done, s32[16384]{0:T(1024)S(1)} %fusion.24), kind=kCustom, calls=%fused_computation | custom fusion | bytes 196608 | tf_op jit(solution)/shard_map/jit(_take)/gather | solution.py:30
  239.5 0.1 multiply_cosine_fusion
  239.7 4.7 fusion.8
  244.3 4.0 fusion.2
  248.4 1.9 multiply_reduce_fusion
  250.3 1.9 fusion.38
  252.2 4.3 fusion.25
  256.5 2.3 fusion
  258.8 1.2 copy.29
  260.1 56.3 %all_to_all.33 = f32[32,2,32,256]{3,2,1,0:T(8,128)S(1)} all-to-all(f32[32,2,32,256]{3,2,1,0:T(8,128)S(1)} %copy.29), channel_id=1, replica_groups=mesh['tile'=8,'freq'=32] {'freq'}, dimensions={0} | all-to-all | bytes 4194304 | tf_op jit(solution)/shard_map/all_to_all | solution.py:60
  316.3 0.2 copy.30
  316.6 1.9 copy-done.1
  318.5 3.8 fusion.14
  322.4 0.2 copy.32
  322.6 4.7 scatter_custom_fusion
  327.3 0.0 all-reduce.6.cloned.1.call-start
  327.3 150.7 %all-reduce.4.cloned.1.call-done = f32[2048,256]{1,0:T(8,128)} async-done(((f32[2048,256]{1,0:T(8,128)}), f32[2048,256]{1,0:T(8,128)}) %all-reduce.4.cloned.1.call-update) | async-done | bytes 2097168 | tf_op jit(solution)/shard_map/psum | solution.py:16
  478.0 73.0 %all-reduce.6.cloned.1.call-done = f32[2048,256]{1,0:T(8,128)} async-done(((f32[2048,256]{1,0:T(8,128)}), f32[2048,256]{1,0:T(8,128)}) %all-reduce.6.cloned.1.call-update) | async-done | bytes 2097168 | tf_op jit(solution)/shard_map/psum | solution.py:16
  551.0 0.7 multiply_reduce_fusion.1
  551.7 78.6 %all-reduce = (f32[256]{0:T(256)S(1)}, f32[256]{0:T(256)S(1)}) all-reduce(f32[256]{0:T(256)S(1)} %get-tuple-element.8, f32[256]{0:T(256)S(1)} %multiply_reduce_fusion.1), channel_id=1, replica_groups=mesh['tile'=8,'freq'=32] {'tile','freq'}, use_global_device_ids=true, to_apply=%region_1.2 | all-reduce | flops 512 | bytes 4096 | tf_op jit(solution)/shard_map/psum | solution.py:56
  630.3 0.6 multiply_multiply_fusion
  630.9 1.3 multiply_subtract_fusion
  (16 shorter events, 0.1 us)
Async XLA Ops:
  7.2 134.9 %copy-start = (f32[128]{0:T(128)S(1)}, f32[128]{0:T(128)}, u32[]{:S(2)}) copy-start(f32[128]{0:T(128)} %param.9) | copy-start | bytes 1540
  7.2 112.9 %all-gather.2.cloned.1.call-start = ((), (), s32[]{:S(2)}) async-start(), calls=%async_computation.2 | async-start | bytes 2105344 | tf_op jit(solution)/shard_map/all_gather | solution.py:46
  134.6 105.1 %all-to-all-start = ((f32[1,2,1024,256]{3,1,0,2:T(2,128)}), f32[1,2,1024,256]{3,1,0,2:T(2,128)S(1)}, u32[]{:S(2)}, u32[]{:S(2)}) async-start(f32[1,2,1024,256]{3,1,0,2:T(2,128)} %copy.25), calls=%async_computation | async-start | bytes 4194304 | tf_op jit(solution)/shard_map/all_to_all | solution.py:50
  142.0 336.0 %all-reduce.4.cloned.1.call-start = ((), (), s32[]{:S(2)}) async-start(), calls=%async_computation.3 | async-start | bytes 4194304 | tf_op jit(solution)/shard_map/psum | solution.py:16
  244.3 4.1 copy-start.3
  244.3 4.1 copy-start.4
  316.3 2.2 copy-start.1
  327.3 303.6 %copy-start.2 = (f32[8,256]{1,0:T(8,128)S(1)}, f32[8,256]{1,0:T(8,128)}, u32[]{:S(2)}) copy-start(f32[8,256]{1,0:T(8,128)} %param.7) | copy-start | bytes 24580
  327.3 223.7 %all-reduce.6.cloned.1.call-start = ((), (), s32[]{:S(2)}) async-start(), calls=%async_computation.4 | async-start | bytes 4194304 | tf_op jit(solution)/shard_map/psum | solution.py:16
Sparse Core Ops, SparseCore 0:
  11.7 108.2 all-gather.1
  327.4 150.5 all-reduce.3
  480.4 70.5 all-reduce.5
